TPU v7x, 256 devices: a whole 4x4x8 slice. The times are simulated.
256 devices in a mesh: grp: 8 (over x_hi, y), blk: 32 (over x_lo, z, core).
Axes of the slice: x: 4 (x_hi: 2, x_lo: 2; x = x_hi * 2 + x_lo), y: 4, z: 8, core: 2. Of those that a mesh axis runs over, the one named last changes fastest.
Arguments:
- queries: bfloat16 [32768, 4096], P(('grp', 'blk')), parts along dimension 0, may hold values from -256 to 256
- new_keys: bfloat16 [32768, 512], P(('grp', 'blk')), parts along dimension 0, may hold values from -6 to 6
- new_values: bfloat16 [32768, 512], P(('grp', 'blk')), parts along dimension 0, may hold values from -6 to 6
- prefix_keys: bfloat16 [32768, 512], P(('grp', 'blk')), parts along dimension 0, may hold values from -6 to 6
- prefix_values: bfloat16 [32768, 512], P(('grp', 'blk')), parts along dimension 0, may hold values from -6 to 6
- block_table: int32 [256, 16], P(('grp', 'blk')), parts along dimension 0, may hold values from 0 to 31, as said below
- prefix_blocks: int32 [256], P(('grp', 'blk')), parts along dimension 0, may hold values from 1 to 16, 320 in all
Outputs:
- attended: bfloat16 [32768, 4096], P(('grp', 'blk')), parts along dimension 0
There are 8 independent parts, one for each index of `grp`. A program takes and returns all parts, laid end to end along the dimension named above; each array names one. Nothing has to cross between parts.
Inputs may be any that keep to these rules, and one draw needn't show every extreme that they name: `block_table`: each row names 16 different prefix blocks; only the first prefix_blocks entries of a row are read. `prefix_blocks`: within each group (each index of grp) the lengths sum to 320.
All inputs are finite; a program needn't handle non-finite values.
Results may differ from a plain program's by a relative error of at most 0.008.
Values may be sent and summed in bfloat16 or wider, within the bound.
No kernel may reach another device: no remote copies, remote signals or barrier semaphores. Data moves between devices by JAX's collectives and lax.ppermute only.
A program may use at most 64 MiB of HBM per device.

v0:
```python
import jax
import jax.numpy as jnp
from jax import lax
from jax.sharding import PartitionSpec as P

KVH = 4
DH = 128
BS = 128
G = 8


def head_major(block, heads):
    rows = block.shape[0]
    return block.reshape(rows, heads, DH).transpose(1, 0, 2)


def absorb(carry, key_block, value_block, usable, query_heads):
    top, total, summed = carry
    scores = jnp.einsum(
        "krd,kld->krl", query_heads, key_block, preferred_element_type=jnp.float32
    ) * DH ** (-0.5)
    scores = jnp.where(usable, scores, -jnp.inf)
    new_top = jnp.maximum(top, jnp.max(scores, axis=-1))
    factor = jnp.exp(top - new_top)
    weights = jnp.exp(scores - new_top[..., None])
    total = factor * total + jnp.sum(weights, axis=-1)
    summed = factor[..., None] * summed + jnp.einsum(
        "krl,kld->krd",
        weights.astype(jnp.bfloat16),
        value_block,
        preferred_element_type=jnp.float32,
    )
    return (new_top, total, summed)


def body(queries, new_keys, new_values, prefix_keys, prefix_values, block_table, prefix_blocks):
    tokens = queries.shape[0]
    query_heads = (
        queries.reshape(tokens, KVH, G, DH).transpose(1, 2, 0, 3).reshape(KVH, G * tokens, DH)
    )
    own_keys = head_major(new_keys, KVH)
    own_values = head_major(new_values, KVH)
    scores = jnp.einsum(
        "krd,kld->krl", query_heads, own_keys, preferred_element_type=jnp.float32
    ) * DH ** (-0.5)
    row_token = jnp.arange(G * tokens, dtype=jnp.int32) % tokens
    causal = jnp.arange(tokens, dtype=jnp.int32)[None, :] <= row_token[:, None]
    scores = jnp.where(causal[None], scores, -jnp.inf)
    top = jnp.max(scores, axis=-1)
    weights = jnp.exp(scores - top[..., None])
    total = jnp.sum(weights, axis=-1)
    summed = jnp.einsum(
        "krl,kld->krd", weights.astype(jnp.bfloat16), own_values, preferred_element_type=jnp.float32
    )
    carry = (top, total, summed)
    table_row = block_table[0]
    length = prefix_blocks[0]
    entries = table_row.shape[0]
    pool_count = lax.axis_size("blk")
    live_entry = jnp.arange(entries, dtype=jnp.int32) < length
    matches = (table_row[None, :] == jnp.arange(pool_count, dtype=jnp.int32)[:, None]) & live_entry[
        None, :
    ]
    used = jnp.any(matches, axis=1)
    state = carry
    piece_keys = lax.all_gather(prefix_keys, "blk", axis=0, tiled=True)
    piece_values = lax.all_gather(prefix_values, "blk", axis=0, tiled=True)
    count = piece_keys.shape[0] // BS
    key_blocks = piece_keys.reshape(count, BS, KVH, DH).transpose(0, 2, 1, 3)
    value_blocks = piece_values.reshape(count, BS, KVH, DH).transpose(0, 2, 1, 3)
    block_ids = jnp.arange(count, dtype=jnp.int32)

    def visit(inner, items):
        key_block, value_block, block_id = items
        return (absorb(inner, key_block, value_block, used[block_id], query_heads), None)

    state, _ = lax.scan(visit, state, (key_blocks, value_blocks, block_ids))
    carry = state
    top, total, summed = carry
    result = summed / total[..., None]
    result = result.reshape(KVH, G, tokens, DH).transpose(2, 0, 1, 3).reshape(tokens, KVH * G * DH)
    return result.astype(jnp.bfloat16)


def solution(mesh):
    in_specs = (
        P(("grp", "blk"), None),
        P(("grp", "blk"), None),
        P(("grp", "blk"), None),
        P(("grp", "blk"), None),
        P(("grp", "blk"), None),
        P(("grp", "blk"), None),
        P(("grp", "blk")),
    )
    out_specs = P(("grp", "blk"), None)
    return jax.shard_map(body, mesh=mesh, in_specs=in_specs, out_specs=out_specs, check_vma=False)
```

profile of v0, /device:TPU:1, one launch (start us, length us, event | category | flops | bytes accessed | tf_op | source)
XLA Modules:
  0.0 444.6 jit_solution(10240727030767275506)
XLA Ops:
  12.5 67.8 %all-gather.5.cloned.1.call-done = bf16[4096,512]{1,0:T(8,128)(2,1)} async-done(((bf16[128,512]{1,0:T(8,128)(2,1)}), bf16[4096,512]{1,0:T(8,128)(2,1)}) %all-gather.5.cloned.1.call-update) | async-done | bytes 4194320 | tf_op jit(solution)/shard_map/all_gather | solution.py:67
  80.3 6.9 %reshape.65 = bf16[32,128,4,128]{3,2,1,0:T(4,128)(2,1)} reshape(bf16[4096,512]{1,0:T(8,128)(2,1)} %all-gather.5.cloned.1.call-done) | data formatting | bytes 8388608 | tf_op jit(solution)/shard_map/reshape | solution.py:70
  87.2 5.3 %copy.57 = bf16[32,128,4,128]{3,1,2,0:T(8,128)(2,1)} copy(bf16[32,128,4,128]{3,2,1,0:T(4,128)(2,1)} %reshape.65) | data formatting | bytes 8388608 | tf_op jit(solution)/shard_map/transpose | solution.py:70
  92.5 56.1 %all-gather.3.cloned.1.call-done = bf16[4096,512]{1,0:T(8,128)(2,1)} async-done(((bf16[128,512]{1,0:T(8,128)(2,1)}), bf16[4096,512]{1,0:T(8,128)(2,1)}) %all-gather.3.cloned.1.call-update) | async-done | bytes 4194320 | tf_op jit(solution)/shard_map/all_gather | solution.py:66
  148.6 6.9 %reshape.64 = bf16[32,128,4,128]{3,2,1,0:T(4,128)(2,1)} reshape(bf16[4096,512]{1,0:T(8,128)(2,1)} %all-gather.3.cloned.1.call-done) | data formatting | bytes 8388608 | tf_op jit(solution)/shard_map/reshape | solution.py:69
  155.6 5.3 %copy.58 = bf16[32,128,4,128]{3,1,2,0:T(8,128)(2,1)} copy(bf16[32,128,4,128]{3,2,1,0:T(4,128)(2,1)} %reshape.64) | data formatting | bytes 8388608 | tf_op jit(solution)/shard_map/transpose | solution.py:69
  160.9 274.0 %while.14 = (s32[]{:T(128)}, f32[4,1024]{1,0:T(4,128)S(1)}, f32[4,1024]{1,0:T(4,128)S(1)}, f32[4,1024,128]{2,1,0:T(8,128)S(1)}, s32[32]{0:T(128)S(1)}, /*index=5...) while((s32[]{:T(128)}, f32[4,1024]{1,0:T(4,128)S(1)}, ...), condition=%wide.region_6.7_spmd, body=%wide.region_3.6_spmd.sunk | while | flops 275259392 | bytes 12060842 | solution.py:77
  166.7 2.7 multiply_add_fusion.5
  172.3 1.9 bitcast_reduce_fusion.2
  175.3 2.7 multiply_add_fusion.5
  180.9 1.9 bitcast_reduce_fusion.2
  183.9 2.7 multiply_add_fusion.5
  189.4 1.9 bitcast_reduce_fusion.2
  192.4 2.7 multiply_add_fusion.5
  198.0 1.9 bitcast_reduce_fusion.2
  201.0 2.7 multiply_add_fusion.5
  206.6 1.9 bitcast_reduce_fusion.2
  209.6 2.7 multiply_add_fusion.5
  215.1 1.9 bitcast_reduce_fusion.2
  218.1 2.7 multiply_add_fusion.5
  223.7 1.9 bitcast_reduce_fusion.2
  226.7 2.7 multiply_add_fusion.5
  232.3 1.9 bitcast_reduce_fusion.2
  235.3 2.7 multiply_add_fusion.5
  240.8 1.9 bitcast_reduce_fusion.2
  243.8 2.7 multiply_add_fusion.5
  252.4 2.7 multiply_add_fusion.5
  260.9 2.7 multiply_add_fusion.5
  269.5 2.7 multiply_add_fusion.5
  278.1 2.7 multiply_add_fusion.5
  286.6 2.7 multiply_add_fusion.5
  295.2 2.7 multiply_add_fusion.5
  303.8 2.7 multiply_add_fusion.5
  312.3 2.7 multiply_add_fusion.5
  320.9 2.7 multiply_add_fusion.5
  329.5 2.7 multiply_add_fusion.5
  338.0 2.7 multiply_add_fusion.5
  346.6 2.7 multiply_add_fusion.5
  355.2 2.7 multiply_add_fusion.5
  363.7 2.7 multiply_add_fusion.5
  372.3 2.7 multiply_add_fusion.5
  380.8 2.7 multiply_add_fusion.5
  389.4 2.7 multiply_add_fusion.5
  398.0 2.7 multiply_add_fusion.5
  406.5 2.7 multiply_add_fusion.5
  415.1 2.7 multiply_add_fusion.5
  423.7 2.7 multiply_add_fusion.5
  432.2 2.7 multiply_add_fusion.5
  (238 shorter events, 121.9 us)
Async XLA Ops:
  6.5 4.2 copy-start
  6.5 73.8 %all-gather.5.cloned.1.call-start = ((), (), s32[]{:S(2)}) async-start(), calls=%async_computation.1 | async-start | bytes 4325376 | tf_op jit(solution)/shard_map/all_gather | solution.py:67
  7.3 141.4 %all-gather.3.cloned.1.call-start = ((), (), s32[]{:S(2)}) async-start(), calls=%async_computation | async-start | bytes 4325376 | tf_op jit(solution)/shard_map/all_gather | solution.py:66
  8.0 2.6 copy-start.2
  10.8 1.0 copy-start.1
Sparse Core Ops, SparseCore 0:
  9.2 71.0 all-gather.4
  82.2 66.4 all-gather.2
where the time goes:
time: 449 us; the launch traced here: 445 us
  matrix products  149 us (33%)
  waiting for transfers between devices  125 us (28%)
  local copies, waits for them, and re-layouts  64.4 us (14%)
  loops' own time  56.5 us (13%)
  other arithmetic  34.9 us (8%)
  between operations  14.2 us (3%)
    dot_general x32, matrix products, absorb(): jnp.einsum('krl,kld->krd', weights.astype(jnp.bfloat16), value_block, pre...  86.5 us
    all_gather x1, waiting for transfers between devices, body(): piece_values = lax.all_gather(prefix_values, 'blk', axis=0, tiled=True)  67.8 us
    dot_general x32, matrix products, absorb(): jnp.einsum('krd,kld->krl', query_heads, key_block, preferred_element_type...  61.6 us
    another operation x1, loops' own time, body(): state, _ = lax.scan(visit, state, (key_blocks, value_blocks, block_ids))  56.5 us
    all_gather x1, waiting for transfers between devices, body(): piece_keys = lax.all_gather(prefix_keys, 'blk', axis=0, tiled=True)  56.1 us
    reduce_sum x32, other arithmetic, absorb(): total = factor * total + jnp.sum(weights, axis=-1)  32.6 us
    dynamic_slice x32, local copies, waits for them, and re-layouts, visit(): used[block_id]  18 us
    dynamic_slice x32, local copies, waits for them, and re-layouts, body(): state, _ = lax.scan(visit, state, (key_blocks, value_blocks, block_ids))  17.9 us
  transfers between devices with their start and end apart: 2, of which 2 were waited for; matrix products, arithmetic and copies ran while one was open for 4% of the time, Pallas kernels for 0%

commit v1 on v0

--- a/solution.py
+++ b/solution.py
@@ -63,7 +63,9 @@
     ]
     used = jnp.any(matches, axis=1)
     state = carry
-    piece_keys = lax.all_gather(prefix_keys, "blk", axis=0, tiled=True)
+    piece_keys = jnp.concatenate(
+        lax.all_to_all(jnp.stack([prefix_keys] * lax.axis_size("blk")), "blk", 0, 0), axis=0
+    )
     piece_values = lax.all_gather(prefix_values, "blk", axis=0, tiled=True)
     count = piece_keys.shape[0] // BS
     key_blocks = piece_keys.reshape(count, BS, KVH, DH).transpose(0, 2, 1, 3)

time: 449 us -> 427 us (0.951)
  waiting for transfers between devices: 125 us -> 97.7 us
  starting transfers between devices: 0.04 us -> 11.2 us
  local copies, waits for them, and re-layouts: 64.4 us -> 54.9 us
    all_gather x1 -> x0, waiting for transfers between devices: 56.1 us -> none  [body(): piece_keys = lax.all_gather(prefix_keys, 'blk', axis=0, tiled=True)]
    all_gather x1, waiting for transfers between devices: 67.8 us -> 93 us  [body(): piece_values = lax.all_gather(prefix_values, 'blk', axis=0, tiled=True)]
    all_to_all x0 -> x1, starting transfers between devices: none -> 11.2 us  [body(): lax.all_to_all(jnp.stack([prefix_keys] * lax.axis_size('blk')), 'blk', 0, 0)]
    reshape x1 -> x0, local copies, waits for them, and re-layouts: 6.93 us -> none  [body(): key_blocks = piece_keys.reshape(count, BS, KVH, DH).transpose(0, 2, 1, 3)]
    transpose x1 -> x0, local copies, waits for them, and re-layouts: 5.33 us -> none  [body(): key_blocks = piece_keys.reshape(count, BS, KVH, DH).transpose(0, 2, 1, 3)]
where the time goes in v1:
time: 427 us; the launch traced here: 421 us
  matrix products  151 us (35%)
  waiting for transfers between devices  97.7 us (23%)
  loops' own time  56.5 us (13%)
  local copies, waits for them, and re-layouts  54.9 us (13%)
  other arithmetic  34.9 us (8%)
  between operations  14.2 us (3%)
  starting transfers between devices  11.2 us (3%)
    all_gather x1, waiting for transfers between devices, body(): piece_values = lax.all_gather(prefix_values, 'blk', axis=0, tiled=True)  93 us
    dot_general x32, matrix products, absorb(): jnp.einsum('krl,kld->krd', weights.astype(jnp.bfloat16), value_block, pre...  86.5 us
    dot_general x32, matrix products, absorb(): jnp.einsum('krd,kld->krl', query_heads, key_block, preferred_element_type...  63.4 us
    another operation x1, loops' own time, body(): state, _ = lax.scan(visit, state, (key_blocks, value_blocks, block_ids))  56.5 us
    reduce_sum x32, other arithmetic, absorb(): total = factor * total + jnp.sum(weights, axis=-1)  32.6 us
    dynamic_slice x32, local copies, waits for them, and re-layouts, visit(): used[block_id]  18 us
    dynamic_slice x32, local copies, waits for them, and re-layouts, body(): state, _ = lax.scan(visit, state, (key_blocks, value_blocks, block_ids))  17.9 us
    all_to_all x1, starting transfers between devices, body(): lax.all_to_all(jnp.stack([prefix_keys] * lax.axis_size('blk')), 'blk', 0, 0)  11.2 us
  transfers between devices with their start and end apart: 2, of which 2 were waited for; matrix products, arithmetic and copies ran while one was open for 4% of the time, Pallas kernels for 0%

profile of v1, /device:TPU:1, one launch (start us, length us, event | category | flops | bytes accessed | tf_op | source)
XLA Modules:
  0.0 420.6 jit_solution(14548416305319080661)
XLA Ops:
  8.3 2.9 stack.2
  11.2 11.2 %all-to-all-start = ((bf16[32,128,512]{1,2,0:T(8,128)(2,1)}), bf16[32,128,512]{1,2,0:T(8,128)(2,1)}, u32[]{:S(2)}, u32[]{:S(2)}) async-start(bf16[32,128,512]{1,2,0:T(8,128)(2,1)} %stack.2), calls=%async_computation | async-start | bytes 8388608 | tf_op jit(solution)/shard_map/all_to_all | solution.py:67
  25.8 93.0 %all-gather.2.cloned.1.call-done = bf16[4096,512]{1,0:T(8,128)(2,1)} async-done(((bf16[128,512]{1,0:T(8,128)(2,1)}), bf16[4096,512]{1,0:T(8,128)(2,1)}) %all-gather.2.cloned.1.call-update) | async-done | bytes 4194320 | tf_op jit(solution)/shard_map/all_gather | solution.py:69
  118.8 6.9 %reshape.62 = bf16[32,128,4,128]{3,2,1,0:T(4,128)(2,1)} reshape(bf16[4096,512]{1,0:T(8,128)(2,1)} %all-gather.2.cloned.1.call-done) | data formatting | bytes 8388608 | tf_op jit(solution)/shard_map/reshape | solution.py:72
  125.7 5.3 %copy.55 = bf16[32,128,4,128]{3,1,2,0:T(8,128)(2,1)} copy(bf16[32,128,4,128]{3,2,1,0:T(4,128)(2,1)} %reshape.62) | data formatting | bytes 8388608 | tf_op jit(solution)/shard_map/transpose | solution.py:72
  131.1 4.0 all-to-all-done
  135.0 275.9 %while.14 = (s32[]{:T(128)}, f32[4,1024]{1,0:T(4,128)S(1)}, f32[4,1024]{1,0:T(4,128)S(1)}, f32[4,1024,128]{2,1,0:T(8,128)S(1)}, s32[32]{0:T(128)S(1)}, /*index=5...) while((s32[]{:T(128)}, f32[4,1024]{1,0:T(4,128)S(1)}, ...), condition=%wide.region_6.7_spmd, body=%wide.region_3.6_spmd.sunk | while | flops 275259392 | bytes 12060842 | solution.py:79
  137.9 2.0 bitcast_reduce_fusion.2
  140.9 2.7 multiply_add_fusion.5
  149.5 2.7 multiply_add_fusion.5
  158.2 2.7 multiply_add_fusion.5
  166.8 2.7 multiply_add_fusion.5
  175.4 2.7 multiply_add_fusion.5
  184.0 2.7 multiply_add_fusion.5
  192.7 2.7 multiply_add_fusion.5
  201.3 2.7 multiply_add_fusion.5
  206.8 2.0 bitcast_reduce_fusion.2
  209.9 2.7 multiply_add_fusion.5
  215.5 2.0 bitcast_reduce_fusion.2
  218.5 2.7 multiply_add_fusion.5
  224.1 2.0 bitcast_reduce_fusion.2
  227.1 2.7 multiply_add_fusion.5
  232.7 2.0 bitcast_reduce_fusion.2
  235.8 2.7 multiply_add_fusion.5
  241.3 2.0 bitcast_reduce_fusion.2
  244.4 2.7 multiply_add_fusion.5
  253.0 2.7 multiply_add_fusion.5
  261.6 2.7 multiply_add_fusion.5
  270.3 2.7 multiply_add_fusion.5
  278.9 2.7 multiply_add_fusion.5
  284.5 2.0 bitcast_reduce_fusion.2
  287.5 2.7 multiply_add_fusion.5
  293.1 2.0 bitcast_reduce_fusion.2
  296.1 2.7 multiply_add_fusion.5
  301.7 2.0 bitcast_reduce_fusion.2
  304.8 2.7 multiply_add_fusion.5
  313.4 2.7 multiply_add_fusion.5
  322.0 2.7 multiply_add_fusion.5
  330.6 2.7 multiply_add_fusion.5
  339.2 2.7 multiply_add_fusion.5
  347.9 2.7 multiply_add_fusion.5
  356.5 2.7 multiply_add_fusion.5
  365.1 2.7 multiply_add_fusion.5
  373.7 2.7 multiply_add_fusion.5
  382.4 2.7 multiply_add_fusion.5
  391.0 2.7 multiply_add_fusion.5
  399.6 2.7 multiply_add_fusion.5
  408.2 2.7 multiply_add_fusion.5
  (239 shorter events, 122.3 us)
Async XLA Ops:
  6.5 17.5 %copy-start = (bf16[128,512]{1,0:T(8,128)(2,1)S(1)}, bf16[128,512]{1,0:T(8,128)(2,1)}, u32[]{:S(2)}) copy-start(bf16[128,512]{1,0:T(8,128)(2,1)} %param.10) | copy-start | bytes 393220
  6.5 112.3 %all-gather.2.cloned.1.call-start = ((), (), s32[]{:S(2)}) async-start(), calls=%async_computation.1 | async-start | bytes 4325376 | tf_op jit(solution)/shard_map/all_gather | solution.py:69
  11.2 11.2 %copy-start.1 = (bf16[128,4096]{1,0:T(8,128)(2,1)S(1)}, bf16[128,4096]{1,0:T(8,128)(2,1)}, u32[]{:S(2)}) copy-start(bf16[128,4096]{1,0:T(8,128)(2,1)} %param.9) | copy-start | bytes 3145732
  11.2 123.8 %all-to-all-start = ((bf16[32,128,512]{1,2,0:T(8,128)(2,1)}), bf16[32,128,512]{1,2,0:T(8,128)(2,1)}, u32[]{:S(2)}, u32[]{:S(2)}) async-start(bf16[32,128,512]{1,2,0:T(8,128)(2,1)} %stack.2), calls=%async_computation | async-start | bytes 8388608 | tf_op jit(solution)/shard_map/all_to_all | solution.py:67
  22.5 1.4 copy-start.3
  24.0 1.0 copy-start.2
Sparse Core Ops, SparseCore 0:
  9.2 109.5 all-gather.1
